TPU v7x, 256 devices: a whole 4x4x8 slice. The times are simulated.
256 devices in a mesh: rep: 32 (over x_hi, z, core), tp: 8 (over x_lo, y).
Axes of the slice: x: 4 (x_hi: 2, x_lo: 2; x = x_hi * 2 + x_lo), y: 4, z: 8, core: 2. Of those that a mesh axis runs over, the one named last changes fastest.
Arguments:
- hidden: bfloat16 [4, 2048, 8192], P(None, 'rep', 'tp'), may hold values from -6 to 6
- query_base: bfloat16 [4, 2048, 8192], P(None, 'rep', 'tp'), may hold values from -13 to 13
- kv_base: bfloat16 [4, 2048, 2, 1024], P(None, 'rep', None, 'tp'), may hold values from -6 to 6
- kv_cache: bfloat16 [2048, 128, 2, 1024], P('rep', None, None, 'tp'), may hold values from -13 to 13
- cache_lengths: int32 [2048], P('rep'), may hold values from 2 to 124
- adapter_ids: int32 [4, 2048], P(None, 'rep'), may hold values from 0 to 5, as said below
- migrating: int32 [4, 64], P(None, 'rep'), may hold values from 0 to 63, as said below
- pair_mask: int32 [4], replicated, may hold values from 1 to 16, as said below
- owners: int32 [4], replicated, may hold values from 0 to 31, as said below
- pool_down: bfloat16 [2, 2, 64, 8192], P(None, None, None, 'tp'), may hold values from -0.0625 to 0.0625
- pool_upq: bfloat16 [2, 64, 8192], P(None, None, 'tp'), may hold values from -0.75 to 0.75
- pool_upv: bfloat16 [2, 64, 1024], P(None, None, 'tp'), may hold values from -0.75 to 0.75
- store_down: bfloat16 [32, 2, 64, 8192], P('rep', None, None, 'tp'), may hold values from -0.0625 to 0.0625
- store_upq: bfloat16 [32, 64, 8192], P('rep', None, 'tp'), may hold values from -0.75 to 0.75
- store_upv: bfloat16 [32, 64, 1024], P('rep', None, 'tp'), may hold values from -0.75 to 0.75
Outputs:
- attention: bfloat16 [4, 2048, 8192], P(None, 'rep', 'tp')
Inputs may be any that keep to these rules, and one draw needn't show every extreme that they name: The 4 owners are distinct replicas. `migrating`: at one step the 2 entries of one replica are distinct slots. `adapter_ids`: at step s every entry is at most 2 + s. `pair_mask`: every entry is a power of two.
All inputs are finite; a program needn't handle non-finite values.
Results may differ from a plain program's by a relative error of at most 0.0064.
Values may be sent and summed in bfloat16 or wider, within the bound.
No kernel may reach another device: no remote copies, remote signals or barrier semaphores. Data moves between devices by JAX's collectives and lax.ppermute only.
A program may use at most 128 MiB of HBM per device.

v0:
```python
import math
import jax
import jax.numpy as jnp
from jax import lax
from jax.sharding import PartitionSpec as P

HD = 128
POOL = 2
STEPS = 4


def from_root(value, axis, source):
    kept = jnp.where(lax.axis_index(axis) == source, value, 0).astype(value.dtype)
    return lax.psum(kept, axis)


def attend(query_rows, kv_rows, lengths, head_dim):
    req_count = kv_rows.shape[0]
    ctx_len = kv_rows.shape[1]
    kv_local = kv_rows.shape[3] // head_dim
    group_size = query_rows.shape[1] // (kv_local * head_dim)
    heads_q = query_rows.reshape(req_count, kv_local, group_size, head_dim)
    key_rows = kv_rows[:, :, 0].reshape(req_count, ctx_len, kv_local, head_dim)
    value_rows = kv_rows[:, :, 1].reshape(req_count, ctx_len, kv_local, head_dim)
    scores = jnp.einsum(
        "rkgd,rckd->rkgc", heads_q, key_rows, preferred_element_type=jnp.float32
    ) / math.sqrt(head_dim)
    valid_mask = jnp.arange(ctx_len)[None, :] <= lengths[:, None]
    scores = jnp.where(valid_mask[:, None, None, :], scores, -1e30)
    row_peak = jnp.max(scores, axis=-1, keepdims=True)
    exp_scores = jnp.exp(scores - row_peak)
    weights = (exp_scores / jnp.sum(exp_scores, axis=-1, keepdims=True)).astype(jnp.bfloat16)
    mixed_out = jnp.einsum(
        "rkgc,rckd->rkgd", weights, value_rows, preferred_element_type=jnp.float32
    )
    return mixed_out.astype(jnp.bfloat16).reshape(req_count, -1)


def local(
    hidden,
    query_base,
    kv_base,
    kv_cache,
    cache_lengths,
    adapter_ids,
    migrating,
    pair_mask,
    owners,
    pool_down,
    pool_upq,
    pool_upv,
    store_down,
    store_upq,
    store_upv,
):
    slots_all = POOL + STEPS
    rep_index = lax.axis_index("rep")
    down_all = jnp.concatenate(
        [pool_down, jnp.zeros((STEPS,) + pool_down.shape[1:], jnp.bfloat16)], axis=0
    )
    upq_all = jnp.concatenate(
        [pool_upq, jnp.zeros((STEPS,) + pool_upq.shape[1:], jnp.bfloat16)], axis=0
    )
    upv_all = jnp.concatenate(
        [pool_upv, jnp.zeros((STEPS,) + pool_upv.shape[1:], jnp.bfloat16)], axis=0
    )
    kv_state = kv_cache
    lengths = cache_lengths
    req_count = kv_cache.shape[0]
    outputs = []
    for step_num in range(STEPS):
        arrived = (
            from_root(store_down[0], "rep", owners[step_num]),
            from_root(store_upq[0], "rep", owners[step_num]),
            from_root(store_upv[0], "rep", owners[step_num]),
        )
        down_all = down_all.at[POOL + step_num].set(arrived[0])
        upq_all = upq_all.at[POOL + step_num].set(arrived[1])
        upv_all = upv_all.at[POOL + step_num].set(arrived[2])
        slot_ids = migrating[step_num]
        moving = kv_state[slot_ids]
        moving_len = lengths[slot_ids].astype(jnp.bfloat16)
        replicas = lax.axis_size("rep")
        partner = jnp.bitwise_xor(rep_index, pair_mask[step_num])
        chosen_slot = jnp.arange(replicas) == partner
        send_rows = jnp.where(
            chosen_slot[:, None, None, None, None], moving[None], jnp.zeros((), jnp.bfloat16)
        )
        send_len = jnp.where(chosen_slot[:, None], moving_len[None], jnp.zeros((), jnp.bfloat16))
        got_rows, got_len = (
            lax.all_to_all(send_rows, "rep", split_axis=0, concat_axis=0, tiled=True),
            lax.all_to_all(send_len, "rep", split_axis=0, concat_axis=0, tiled=True),
        )
        moving = got_rows[partner]
        moving_len = got_len[partner]
        kv_state = kv_state.at[slot_ids].set(moving)
        lengths = lengths.at[slot_ids].set(moving_len.astype(jnp.int32))
        tokens = hidden[step_num]
        partial_sum = jnp.einsum(
            "rd,apkd->rapk", tokens, down_all, preferred_element_type=jnp.float32
        )
        picker = (adapter_ids[step_num][:, None] == jnp.arange(slots_all)[None, :]).astype(
            jnp.float32
        )
        summed = lax.psum(partial_sum, "tp")
        low_rank = jnp.sum(picker[:, :, None, None] * summed, axis=1)
        low_rank = low_rank.astype(jnp.bfloat16)
        spread = picker.astype(jnp.bfloat16)[:, :, None, None] * low_rank[:, None]
        spread_q = spread[:, :, 0].reshape(req_count, -1)
        spread_v = spread[:, :, 1].reshape(req_count, -1)
        delta_q = jnp.dot(
            spread_q, upq_all.reshape(-1, upq_all.shape[2]), preferred_element_type=jnp.float32
        )
        delta_v = jnp.dot(
            spread_v, upv_all.reshape(-1, upv_all.shape[2]), preferred_element_type=jnp.float32
        )
        query_rows = (query_base[step_num].astype(jnp.float32) + delta_q).astype(jnp.bfloat16)
        new_value = (kv_base[step_num][:, 1].astype(jnp.float32) + delta_v).astype(jnp.bfloat16)
        fresh_rows = jnp.stack([kv_base[step_num][:, 0], new_value], axis=1)
        kv_state = kv_state.at[jnp.arange(req_count), lengths].set(fresh_rows)
        outputs.append(attend(query_rows, kv_state, lengths, HD))
        lengths = lengths + 1
    return jnp.stack(outputs, axis=0)


def solution(mesh):
    return jax.shard_map(
        local,
        mesh=mesh,
        in_specs=(
            P(None, "rep", "tp"),
            P(None, "rep", "tp"),
            P(None, "rep", None, "tp"),
            P("rep", None, None, "tp"),
            P("rep"),
            P(None, "rep"),
            P(None, "rep"),
            P(),
            P(),
            P(None, None, None, "tp"),
            P(None, None, "tp"),
            P(None, None, "tp"),
            P("rep", None, None, "tp"),
            P("rep", None, "tp"),
            P("rep", None, "tp"),
        ),
        out_specs=P(None, "rep", "tp"),
        check_vma=False,
    )
```

profile of v0, /device:TPU:1, one launch (start us, length us, event | category | flops | bytes accessed | tf_op | source)
XLA Modules:
  0.0 1123.3 jit_solution(8069463580083351117)
XLA Ops:
  7.2 10.3 copy.207
  20.5 12.6 %all-to-all-start = ((bf16[32,1,2]{2,1,0:T(2,128)(2,1)}), bf16[32,1,2]{2,1,0:T(2,128)(2,1)S(1)}, u32[]{:S(2)}, u32[]{:S(2)}) async-start(bf16[32,1,2]{2,1,0:T(2,128)(2,1)} %broadcast_select_fusion.15), calls=%async_computation | async-start | bytes 32768 | tf_op jit(solution)/shard_map/all_to_all | solution.py:92
  33.7 3.0 gather_fusion.1
  36.8 5.6 all-to-all-done
  44.3 4.3 all-to-all-start.2
  48.6 2.3 broadcast_select_fusion.3
  51.0 7.1 all-to-all-done.2
  58.0 5.2 all-to-all-start.1
  67.4 1.0 broadcast_select_fusion.4
  70.4 287.7 %all-reduce.14.cloned.1.call-done = (bf16[1,2,64,1024]{3,2,1,0:T(8,128)(2,1)}, bf16[1,2,64,1024]{3,2,1,0:T(8,128)(2,1)}, bf16[1,2,64,1024]{3,2,1,0:T(8,128)(2,1)...) async-done(((bf16[1,2,64,1024]{3,2,1,0:T(8,128)(2,1)}, ...) | async-done | bytes 1572880 | tf_op jit(solution)/shard_map/psum | solution.py:14
  358.2 1.0 constant_dynamic-update-slice_fusion.11
  359.2 1.3 convolution_bitcast_fusion.3
  360.5 1.0 constant_dynamic-update-slice_fusion.8
  361.5 1.3 convolution_bitcast_fusion.2
  362.8 1.3 convolution_bitcast_fusion.1
  364.2 1.3 convolution_bitcast_fusion
  367.5 227.4 %all-reduce.12.cloned.1.call-done = (bf16[1,64,128]{2,1,0:T(8,128)(2,1)}, bf16[1,64,128]{2,1,0:T(8,128)(2,1)}, bf16[1,64,128]{2,1,0:T(8,128)(2,1)}, bf16[1,64,128]{2,1,0:T(8,128)(2,1)}) async-done(((bf16[1,64,128]{2,1,0:T(8,128)(2,1)}, bf16[1,64,128]{2,1,0:T(8,128)(2,1)}, bf16[1,64,128]{2,1,0:T(8,128)(2,1)}, bf16[1,64,128]{2,1,0:T(8,128)(2,1)}), (bf16[1,64,128]{2,1,0:T(8,128)(2,1)}, ...) | async-done | bytes 65552 | tf_op jit(solution)/shard_map/psum | solution.py:14
  595.6 79.9 %all-reduce.10.cloned.1.call-done = (f32[64,6,2,64]{0,3,2,1:T(8,128)}, f32[64,6,2,64]{0,3,2,1:T(8,128)}, f32[64,6,2,64]{0,3,2,1:T(8,128)}, f32[64,6,2,64]{0,3,2,1:T(8,128)}) async-done(((f32[64,6,2,64]{0,3,2,1:T(8,128)}, f32[64,6,2,64]{0,3,2,1:T(8,128)}, f32[64,6,2,64]{0,3,2,1:T(8,128)}, f32[64,6,2,64]{0,3,2,1:T(8,128)}), (f32[64,6,2,64]{0,3,2,1:T(8,128)}, f32[64,6,2,64]{0,3,2,1:T(8,128)}, ...) | async-done | bytes 786448 | tf_op jit(solution)/shard_map/psum | solution.py:105
  675.5 1.2 multiply_reduce_fusion.2
  677.3 14.0 %all-to-all-start.4 = ((bf16[32,1,2]{2,1,0:T(2,128)(2,1)}), bf16[32,1,2]{2,1,0:T(2,128)(2,1)S(1)}, u32[]{:S(2)}, u32[]{:S(2)}) async-start(bf16[32,1,2]{2,1,0:T(2,128)(2,1)} %broadcast_select_fusion.13), calls=%async_computation.4 | async-start | bytes 32768 | tf_op jit(solution)/shard_map/all_to_all | solution.py:92
  691.3 0.9 constant_dynamic-slice_fusion.3
  692.4 2.2 scatter_fusion.1
  694.6 8.0 scatter_fusion.2
  702.5 3.0 gather_fusion.3
  705.6 2.3 broadcast_select_fusion.2
  707.9 10.1 all-to-all-start.3
  721.4 5.3 copy.75
  726.7 87.4 %all-to-all-done.3 = bf16[32,2,128,2,128]{4,2,3,1,0:T(8,128)(2,1)} async-done(((bf16[32,2,128,2,128]{4,2,3,1,0:T(8,128)(2,1)}), bf16[32,2,128,2,128]{4,2,3,1,0:T(8,128)(2,1)}, u32[]{:S(2)}, u32[]{:S(2)}) %all-to-all-start.3) | async-done | bytes 4194336 | tf_op jit(solution)/shard_map/all_to_all | solution.py:91
  814.2 7.1 all-to-all-start.6
  821.2 0.9 dynamic-slice_bitcast_fusion.2
  822.2 2.1 scatter_fusion.4
  824.2 8.5 copy.77
  832.7 8.0 scatter_fusion.5
  840.7 3.0 gather_fusion.5
  843.7 2.3 broadcast_select_fusion.1
  846.0 10.1 all-to-all-start.5
  858.4 5.3 copy.84
  863.7 88.7 %all-to-all-done.5 = bf16[32,2,128,2,128]{4,2,3,1,0:T(8,128)(2,1)} async-done(((bf16[32,2,128,2,128]{4,2,3,1,0:T(8,128)(2,1)}), bf16[32,2,128,2,128]{4,2,3,1,0:T(8,128)(2,1)}, u32[]{:S(2)}, u32[]{:S(2)}) %all-to-all-start.5) | async-done | bytes 4194336 | tf_op jit(solution)/shard_map/all_to_all | solution.py:91
  952.4 0.9 dynamic-slice_bitcast_fusion.1
  953.3 2.1 scatter_fusion.7
  955.4 8.5 copy.86
  963.9 7.9 scatter_fusion.8
  971.8 3.0 gather_fusion.7
  974.8 2.3 broadcast_select_fusion
  977.2 7.8 all-to-all-start.7
  987.6 9.9 fusion.93
  997.6 1.2 fusion.17
  999.0 3.1 fusion.32
  1002.2 10.0 fusion.94
  1012.2 1.2 fusion.19
  1013.6 3.1 fusion.33
  1016.8 5.4 copy.93
  1022.2 6.8 fusion.95
  1029.0 1.2 fusion.21
  1030.4 3.1 fusion.34
  1033.6 47.4 %all-to-all-done.7 = bf16[32,2,128,2,128]{4,2,3,1,0:T(8,128)(2,1)} async-done(((bf16[32,2,128,2,128]{4,2,3,1,0:T(8,128)(2,1)}), bf16[32,2,128,2,128]{4,2,3,1,0:T(8,128)(2,1)}, u32[]{:S(2)}, u32[]{:S(2)}) %all-to-all-start.7) | async-done | bytes 4194336 | tf_op jit(solution)/shard_map/all_to_all | solution.py:91
  1081.0 0.9 dynamic-slice_bitcast_fusion
  1081.9 2.3 scatter_fusion.10
  1084.3 8.5 copy.95
  1092.8 8.0 scatter_fusion.11
  1100.8 10.0 fusion.96
  1110.8 1.2 fusion.23
  1112.2 3.1 fusion.35
  1115.4 0.9 pad_maximum_fusion
  (189 shorter events, 19.7 us)
Async XLA Ops:
  7.2 10.4 copy-start.22
  7.2 11.7 %copy-start.17 = (s32[4,2]{0,1:T(2,128)S(1)}, s32[4,2]{0,1:T(2,128)}, u32[]{:S(2)}) copy-start(s32[4,2]{0,1:T(2,128)} %param.45) | copy-start | bytes 100
  20.5 21.9 %all-to-all-start = ((bf16[32,1,2]{2,1,0:T(2,128)(2,1)}), bf16[32,1,2]{2,1,0:T(2,128)(2,1)S(1)}, u32[]{:S(2)}, u32[]{:S(2)}) async-start(bf16[32,1,2]{2,1,0:T(2,128)(2,1)} %broadcast_select_fusion.15), calls=%async_computation | async-start | bytes 32768 | tf_op jit(solution)/shard_map/all_to_all | solution.py:92
  44.3 13.7 %all-to-all-start.2 = ((bf16[32,1,2]{2,1,0:T(2,128)(2,1)}), bf16[32,1,2]{2,1,0:T(2,128)(2,1)S(1)}, u32[]{:S(2)}, u32[]{:S(2)}) async-start(bf16[32,1,2]{2,1,0:T(2,128)(2,1)} %broadcast_select_fusion.14), calls=%async_computation.2 | async-start | bytes 32768 | tf_op jit(solution)/shard_map/all_to_all | solution.py:92
  50.9 12.4 %copy-start.23 = (s32[4]{0:T(128)S(1)}, s32[4]{0:T(128)}, u32[]{:S(2)}) copy-start(s32[4]{0:T(128)} %param.47) | copy-start | bytes 52
  50.9 15.6 %copy-start.10 = (bf16[1,64,1024]{2,1,0:T(8,128)(2,1)S(1)}, bf16[1,64,1024]{2,1,0:T(8,128)(2,1)}, u32[]{:S(2)}) copy-start(bf16[1,64,1024]{2,1,0:T(8,128)(2,1)} %param.52) | copy-start | bytes 393220
  50.9 16.5 %copy-start.6 = (bf16[1,2,64,1024]{3,2,1,0:T(8,128)(2,1)S(1)}, bf16[1,2,64,1024]{3,2,1,0:T(8,128)(2,1)}, u32[]{:S(2)}) copy-start(bf16[1,2,64,1024]{3,2,1,0:T(8,128)(2,1)} %param.51) | copy-start | bytes 786436
  50.9 17.5 %copy-start.21 = (bf16[1,64,128]{2,1,0:T(8,128)(2,1)S(1)}, bf16[1,64,128]{2,1,0:T(8,128)(2,1)}, u32[]{:S(2)}) copy-start(bf16[1,64,128]{2,1,0:T(8,128)(2,1)} %param.53) | copy-start | bytes 49156
  50.9 18.3 %copy-start.24 = (s32[4,64]{1,0:T(4,128)S(1)}, s32[4,64]{1,0:T(4,128)}, u32[]{:S(2)}) copy-start(s32[4,64]{1,0:T(4,128)} %param.44) | copy-start | bytes 3076
  51.0 18.4 %copy-start.1 = (bf16[2,2,64,1024]{3,2,1,0:T(8,128)(2,1)S(1)}, bf16[2,2,64,1024]{3,2,1,0:T(8,128)(2,1)}, u32[]{:S(2)}) copy-start(bf16[2,2,64,1024]{3,2,1,0:T(8,128)(2,1)} %param.48) | copy-start | bytes 1572868
  58.0 619.3 %all-to-all-start.1 = ((bf16[32,2,128,2,128]{4,2,3,1,0:T(8,128)(2,1)}), bf16[32,2,128,2,128]{4,2,3,1,0:T(8,128)(2,1)}, u32[]{:S(2)}, u32[]{:S(2)}) async-start(bf16[32,2,128,2,128]{4,2,3,1,0:T(8,128)(2,1)} %broadcast_select_fusion.3), calls=%async_computation.1 | async-start | bytes 8388608 | tf_op jit(solution)/shard_map/all_to_all | solution.py:91
  63.3 6.3 copy-start.16
  63.3 6.3 copy-start.11
  63.3 295.9 %copy-start.2 = (bf16[4,64,1024]{2,1,0:T(8,128)(2,1)S(1)}, bf16[4,64,1024]{2,1,0:T(8,128)(2,1)}, u32[]{:S(2)}) copy-start(bf16[4,64,1024]{2,1,0:T(8,128)(2,1)} %param.39) | copy-start | bytes 1572868
  63.3 294.9 %all-reduce.14.cloned.1.call-start = ((), (), s32[]{:S(2)}) async-start(), calls=%async_computation.10 | async-start | bytes 3145728 | tf_op jit(solution)/shard_map/psum | solution.py:14
  68.4 526.5 %all-reduce.12.cloned.1.call-start = ((), (), s32[]{:S(2)}) async-start(), calls=%async_computation.9 | async-start | bytes 131072 | tf_op jit(solution)/shard_map/psum | solution.py:14
  69.2 606.3 %all-reduce.10.cloned.1.call-start = ((), (), s32[]{:S(2)}) async-start(), calls=%async_computation.8 | async-start | bytes 3145728 | tf_op jit(solution)/shard_map/psum | solution.py:105
  358.2 4.7 copy-start.8
  358.2 6.0 copy-start.7
  677.3 30.6 %all-to-all-start.4 = ((bf16[32,1,2]{2,1,0:T(2,128)(2,1)}), bf16[32,1,2]{2,1,0:T(2,128)(2,1)S(1)}, u32[]{:S(2)}, u32[]{:S(2)}) async-start(bf16[32,1,2]{2,1,0:T(2,128)(2,1)} %broadcast_select_fusion.13), calls=%async_computation.4 | async-start | bytes 32768 | tf_op jit(solution)/shard_map/all_to_all | solution.py:92
  707.9 13.3 %copy-start.20 = (bf16[1,64,128]{2,1,0:T(8,128)(2,1)S(1)}, bf16[1,64,128]{2,1,0:T(8,128)(2,1)}, u32[]{:S(2)}) copy-start(bf16[1,64,128]{2,1,0:T(8,128)(2,1)} %get-tuple-element.158) | copy-start | bytes 49156
  707.9 106.3 %all-to-all-start.3 = ((bf16[32,2,128,2,128]{4,2,3,1,0:T(8,128)(2,1)}), bf16[32,2,128,2,128]{4,2,3,1,0:T(8,128)(2,1)}, u32[]{:S(2)}, u32[]{:S(2)}) async-start(bf16[32,2,128,2,128]{4,2,3,1,0:T(8,128)(2,1)} %broadcast_select_fusion.2), calls=%async_computation.3 | async-start | bytes 8388608 | tf_op jit(solution)/shard_map/all_to_all | solution.py:91
  814.2 31.9 %all-to-all-start.6 = ((bf16[32,1,2]{2,1,0:T(2,128)(2,1)}), bf16[32,1,2]{2,1,0:T(2,128)(2,1)S(1)}, u32[]{:S(2)}, u32[]{:S(2)}) async-start(bf16[32,1,2]{2,1,0:T(2,128)(2,1)} %broadcast_select_fusion.12), calls=%async_computation.6 | async-start | bytes 32768 | tf_op jit(solution)/shard_map/all_to_all | solution.py:92
  846.0 10.1 copy-start.9
  846.0 11.6 %copy-start.4 = (f32[64,6,2,64]{0,3,2,1:T(8,128)S(1)}, f32[64,6,2,64]{0,3,2,1:T(8,128)}, u32[]{:S(2)}) copy-start(f32[64,6,2,64]{0,3,2,1:T(8,128)} %get-tuple-element.155) | copy-start | bytes 589828
  846.0 11.6 %copy-start.5 = (f32[64,6,2,64]{0,3,2,1:T(8,128)S(1)}, f32[64,6,2,64]{0,3,2,1:T(8,128)}, u32[]{:S(2)}) copy-start(f32[64,6,2,64]{0,3,2,1:T(8,128)} %get-tuple-element.156) | copy-start | bytes 589828
  846.0 106.3 %all-to-all-start.5 = ((bf16[32,2,128,2,128]{4,2,3,1,0:T(8,128)(2,1)}), bf16[32,2,128,2,128]{4,2,3,1,0:T(8,128)(2,1)}, u32[]{:S(2)}, u32[]{:S(2)}) async-start(bf16[32,2,128,2,128]{4,2,3,1,0:T(8,128)(2,1)} %broadcast_select_fusion.1), calls=%async_computation.5 | async-start | bytes 8388608 | tf_op jit(solution)/shard_map/all_to_all | solution.py:91
  856.2 2.0 copy-start.19
  977.2 7.9 copy-start.15
  977.2 8.1 copy-start.3
  977.2 8.6 copy-start.14
  977.2 9.0 copy-start.13
  977.2 103.9 %all-to-all-start.7 = ((bf16[32,2,128,2,128]{4,2,3,1,0:T(8,128)(2,1)}), bf16[32,2,128,2,128]{4,2,3,1,0:T(8,128)(2,1)}, u32[]{:S(2)}, u32[]{:S(2)}) async-start(bf16[32,2,128,2,128]{4,2,3,1,0:T(8,128)(2,1)} %broadcast_select_fusion), calls=%async_computation.7 | async-start | bytes 8388608 | tf_op jit(solution)/shard_map/all_to_all | solution.py:91
  985.0 2.0 copy-start.18
  985.0 2.3 copy-start.12
  1016.8 5.4 copy-start
Sparse Core Ops, SparseCore 0:
  68.5 289.5 all-reduce.13
  361.1 233.7 all-reduce.11
  597.8 77.6 all-reduce.9
where the time goes:
time: 1130 us; the launch traced here: 1120 us
  waiting for transfers between devices  831 us (74%)
  local copies, waits for them, and re-layouts  158 us (14%)
  starting transfers between devices  71.2 us (6%)
  matrix products  24.1 us (2%)
  between operations  19.8 us (2%)
  other arithmetic  18.8 us (2%)
    psum x2, waiting for transfers between devices, from_root(): return lax.psum(kept, axis)  515 us
    all_to_all x4, waiting for transfers between devices, local(): lax.all_to_all(send_rows, 'rep', split_axis=0, concat_axis=0, tiled=True)  224 us
    psum x1, waiting for transfers between devices, local(): summed = lax.psum(partial_sum, 'tp')  79.9 us
    scatter x7, local copies, waits for them, and re-layouts, local(): kv_state = kv_state.at[jnp.arange(req_count), lengths].set(fresh_rows)  47.9 us
    all_to_all x4, starting transfers between devices, local(): lax.all_to_all(send_len, 'rep', split_axis=0, concat_axis=0, tiled=True)  37.9 us
    slice x4, local copies, waits for them, and re-layouts, attend(): key_rows = kv_rows[:, :, 0].reshape(req_count, ctx_len, kv_local, head_dim)  36.7 us
    scatter x7, local copies, waits for them, and re-layouts, local(): kv_state = kv_state.at[slot_ids].set(moving)  34.2 us
    all_to_all x4, starting transfers between devices, local(): lax.all_to_all(send_rows, 'rep', split_axis=0, concat_axis=0, tiled=True)  33.2 us
  transfers between devices with their start and end apart: 11, of which 8 were waited for; matrix products, arithmetic and copies ran while one was open for 11% of the time, Pallas kernels for 0%

commit v1 on v0

--- a/solution.py
+++ b/solution.py
@@ -102,7 +102,7 @@
         picker = (adapter_ids[step_num][:, None] == jnp.arange(slots_all)[None, :]).astype(
             jnp.float32
         )
-        summed = lax.psum(partial_sum, "tp")
+        summed = jnp.sum(lax.all_gather(partial_sum, "tp"), axis=0)
         low_rank = jnp.sum(picker[:, :, None, None] * summed, axis=1)
         low_rank = low_rank.astype(jnp.bfloat16)
         spread = picker.astype(jnp.bfloat16)[:, :, None, None] * low_rank[:, None]

time: 1130 us -> 1100 us (0.973)
  waiting for transfers between devices: 831 us -> 774 us
  other arithmetic: 18.8 us -> 34.9 us
    all_gather x0 -> x4, waiting for transfers between devices: none -> 168 us  [local(): summed = jnp.sum(lax.all_gather(partial_sum, 'tp'), axis=0)]
    all_to_all x4, waiting for transfers between devices: 224 us -> 73.8 us  [local(): lax.all_to_all(send_rows, 'rep', split_axis=0, concat_axis=0, tiled=True)]
    psum x1 -> x0, waiting for transfers between devices: 79.9 us -> none  [local(): summed = lax.psum(partial_sum, 'tp')]
    reduce_sum x0 -> x4, other arithmetic: none -> 13.7 us  [local(): summed = jnp.sum(lax.all_gather(partial_sum, 'tp'), axis=0)]
  transfers between devices with their start and end apart: 11 -> 14, of which waited for: 8 -> 10; matrix products, arithmetic and copies ran while one was open for 11% -> 16% of each run, Pallas kernels for 0% -> 0%
where the time goes in v1:
time: 1100 us; the launch traced here: 1090 us
  waiting for transfers between devices  774 us (70%)
  local copies, waits for them, and re-layouts  168 us (15%)
  starting transfers between devices  70 us (6%)
  other arithmetic  34.9 us (3%)
  matrix products  21 us (2%)
  between operations  20.2 us (2%)
    psum x2, waiting for transfers between devices, from_root(): return lax.psum(kept, axis)  519 us
    all_gather x4, waiting for transfers between devices, local(): summed = jnp.sum(lax.all_gather(partial_sum, 'tp'), axis=0)  168 us
    all_to_all x4, waiting for transfers between devices, local(): lax.all_to_all(send_rows, 'rep', split_axis=0, concat_axis=0, tiled=True)  73.8 us
    scatter x7, local copies, waits for them, and re-layouts, local(): kv_state = kv_state.at[jnp.arange(req_count), lengths].set(fresh_rows)  48.2 us
    all_to_all x4, starting transfers between devices, local(): lax.all_to_all(send_len, 'rep', split_axis=0, concat_axis=0, tiled=True)  36.9 us
    slice x4, local copies, waits for them, and re-layouts, attend(): key_rows = kv_rows[:, :, 0].reshape(req_count, ctx_len, kv_local, head_dim)  36.8 us
    scatter x7, local copies, waits for them, and re-layouts, local(): kv_state = kv_state.at[slot_ids].set(moving)  34.2 us
    all_to_all x4, starting transfers between devices, local(): lax.all_to_all(send_rows, 'rep', split_axis=0, concat_axis=0, tiled=True)  32.9 us
  transfers between devices with their start and end apart: 14, of which 10 were waited for; matrix products, arithmetic and copies ran while one was open for 16% of the time, Pallas kernels for 0%

profile of v1, /device:TPU:1, one launch (start us, length us, event | category | flops | bytes accessed | tf_op | source)
XLA Modules:
  0.0 1088.5 jit_solution(3324481511305336987)
XLA Ops:
  7.2 10.4 copy.246
  20.5 12.6 %all-to-all-start = ((bf16[32,1,2]{2,1,0:T(2,128)(2,1)}), bf16[32,1,2]{2,1,0:T(2,128)(2,1)S(1)}, u32[]{:S(2)}, u32[]{:S(2)}) async-start(bf16[32,1,2]{2,1,0:T(2,128)(2,1)} %broadcast_select_fusion.15), calls=%async_computation | async-start | bytes 32768 | tf_op jit(solution)/shard_map/all_to_all | solution.py:92
  33.7 3.0 gather_fusion.1
  36.8 5.6 all-to-all-done
  44.3 4.3 all-to-all-start.2
  48.6 2.3 broadcast_select_fusion.3
  50.9 7.1 all-to-all-done.2
  58.0 5.2 all-to-all-start.1
  67.5 1.0 broadcast_select_fusion.4
  69.5 289.0 %all-reduce.10.cloned.1.call-done = (bf16[1,2,64,1024]{3,2,1,0:T(8,128)(2,1)}, bf16[1,2,64,1024]{3,2,1,0:T(8,128)(2,1)}, bf16[1,2,64,1024]{3,2,1,0:T(8,128)(2,1)...) async-done(((bf16[1,2,64,1024]{3,2,1,0:T(8,128)(2,1)}, ...) | async-done | bytes 1572880 | tf_op jit(solution)/shard_map/psum | solution.py:14
  358.5 1.0 constant_dynamic-update-slice_fusion.11
  365.2 230.0 %all-reduce.8.cloned.1.call-done = (bf16[1,64,128]{2,1,0:T(8,128)(2,1)}, bf16[1,64,128]{2,1,0:T(8,128)(2,1)}, bf16[1,64,128]{2,1,0:T(8,128)(2,1)}, bf16[1,64,128]{2,1,0:T(8,128)(2,1)}) async-done(((bf16[1,64,128]{2,1,0:T(8,128)(2,1)}, bf16[1,64,128]{2,1,0:T(8,128)(2,1)}, bf16[1,64,128]{2,1,0:T(8,128)(2,1)}, bf16[1,64,128]{2,1,0:T(8,128)(2,1)}), (bf16[1,64,128]{2,1,0:T(8,128)(2,1)}, ...) | async-done | bytes 65552 | tf_op jit(solution)/shard_map/psum | solution.py:14
  595.9 42.2 %all-gather.9.cloned.1.call-done = f32[512,6,2,64]{3,2,1,0:T(2,128)} async-done(((f32[64,6,2,64]{3,2,1,0:T(2,128)}), f32[512,6,2,64]{3,2,1,0:T(2,128)}) %all-gather.9.cloned.1.call-update) | async-done | bytes 1572880 | tf_op jit(solution)/shard_map/all_gather | solution.py:105
  638.1 3.4 reduce_sum.108
  642.5 12.6 %all-to-all-start.4 = ((bf16[32,1,2]{2,1,0:T(2,128)(2,1)}), bf16[32,1,2]{2,1,0:T(2,128)(2,1)S(1)}, u32[]{:S(2)}, u32[]{:S(2)}) async-start(bf16[32,1,2]{2,1,0:T(2,128)(2,1)} %broadcast_select_fusion.13), calls=%async_computation.4 | async-start | bytes 32768 | tf_op jit(solution)/shard_map/all_to_all | solution.py:92
  655.1 0.9 constant_dynamic-slice_fusion.3
  656.2 2.2 scatter_fusion.1
  658.3 8.0 scatter_fusion.2
  666.3 3.0 gather_fusion.3
  669.3 2.3 broadcast_select_fusion.2
  671.6 10.0 all-to-all-start.3
  686.0 66.9 %all-gather.11.cloned.1.call-done = f32[512,6,2,64]{3,2,1,0:T(2,128)} async-done(((f32[64,6,2,64]{3,2,1,0:T(2,128)}), f32[512,6,2,64]{3,2,1,0:T(2,128)}) %all-gather.11.cloned.1.call-update) | async-done | bytes 1572880 | tf_op jit(solution)/shard_map/all_gather | solution.py:105
  752.9 3.4 reduce_sum.111
  757.9 5.3 copy.110
  763.2 14.7 %all-to-all-done.3 = bf16[32,2,128,2,128]{4,2,3,1,0:T(8,128)(2,1)} async-done(((bf16[32,2,128,2,128]{4,2,3,1,0:T(8,128)(2,1)}), bf16[32,2,128,2,128]{4,2,3,1,0:T(8,128)(2,1)}, u32[]{:S(2)}, u32[]{:S(2)}) %all-to-all-start.3) | async-done | bytes 4194336 | tf_op jit(solution)/shard_map/all_to_all | solution.py:91
  777.9 7.4 all-to-all-start.6
  785.3 0.9 dynamic-slice_bitcast_fusion.2
  786.2 2.1 scatter_fusion.4
  788.3 8.5 copy.112
  796.8 8.0 scatter_fusion.5
  804.8 3.1 gather_fusion.5
  807.9 2.3 broadcast_select_fusion.1
  810.8 10.0 all-to-all-start.5
  822.5 1.0 concatenate.46
  831.6 1.1 scatter_fusion.9
  832.8 59.1 %all-gather.13.cloned.1.call-done = f32[512,6,2,64]{3,2,1,0:T(2,128)} async-done(((f32[64,6,2,64]{3,2,1,0:T(2,128)}), f32[512,6,2,64]{3,2,1,0:T(2,128)}) %all-gather.13.cloned.1.call-update) | async-done | bytes 1572880 | tf_op jit(solution)/shard_map/all_gather | solution.py:105
  891.9 3.4 reduce_sum.114
  896.3 5.3 copy.121
  901.5 15.5 %all-to-all-done.5 = bf16[32,2,128,2,128]{4,2,3,1,0:T(8,128)(2,1)} async-done(((bf16[32,2,128,2,128]{4,2,3,1,0:T(8,128)(2,1)}), bf16[32,2,128,2,128]{4,2,3,1,0:T(8,128)(2,1)}, u32[]{:S(2)}, u32[]{:S(2)}) %all-to-all-start.5) | async-done | bytes 4194336 | tf_op jit(solution)/shard_map/all_to_all | solution.py:91
  917.0 0.9 dynamic-slice_bitcast_fusion.1
  917.9 2.1 scatter_fusion.7
  920.0 8.6 copy.123
  928.6 8.1 scatter_fusion.8
  936.7 3.2 gather_fusion.7
  939.9 2.3 broadcast_select_fusion
  942.2 7.7 all-to-all-start.7
  951.4 3.4 reduce_sum.117
  956.3 10.0 fusion.93
  966.3 1.2 fusion.17
  967.7 3.1 fusion.32
  970.9 10.0 fusion.94
  980.9 1.2 fusion.19
  982.3 3.1 fusion.33
  985.5 5.4 copy.132
  990.9 6.8 fusion.95
  997.7 1.2 fusion.21
  999.1 3.1 fusion.34
  1002.3 43.6 %all-to-all-done.7 = bf16[32,2,128,2,128]{4,2,3,1,0:T(8,128)(2,1)} async-done(((bf16[32,2,128,2,128]{4,2,3,1,0:T(8,128)(2,1)}), bf16[32,2,128,2,128]{4,2,3,1,0:T(8,128)(2,1)}, u32[]{:S(2)}, u32[]{:S(2)}) %all-to-all-start.7) | async-done | bytes 4194336 | tf_op jit(solution)/shard_map/all_to_all | solution.py:91
  1046.9 2.3 scatter_fusion.10
  1049.2 8.5 copy.134
  1057.7 8.2 scatter_fusion.11
  1065.9 10.1 fusion.96
  1075.9 1.2 fusion.23
  1077.3 3.1 fusion.35
  (266 shorter events, 36.0 us)
Async XLA Ops:
  7.2 10.4 copy-start.41
  7.2 11.7 %copy-start.29 = (s32[4,2]{0,1:T(2,128)S(1)}, s32[4,2]{0,1:T(2,128)}, u32[]{:S(2)}) copy-start(s32[4,2]{0,1:T(2,128)} %param.45) | copy-start | bytes 100
  19.1 344.1 %copy-start.37 = (s32[2]{0:T(128)}, s32[2]{0:T(128)S(1)}, u32[]{:S(2)}) copy-start(s32[2]{0:T(128)S(1)} %get-tuple-element.218) | copy-start | bytes 28
  20.5 21.9 %all-to-all-start = ((bf16[32,1,2]{2,1,0:T(2,128)(2,1)}), bf16[32,1,2]{2,1,0:T(2,128)(2,1)S(1)}, u32[]{:S(2)}, u32[]{:S(2)}) async-start(bf16[32,1,2]{2,1,0:T(2,128)(2,1)} %broadcast_select_fusion.15), calls=%async_computation | async-start | bytes 32768 | tf_op jit(solution)/shard_map/all_to_all | solution.py:92
  44.3 13.7 %all-to-all-start.2 = ((bf16[32,1,2]{2,1,0:T(2,128)(2,1)}), bf16[32,1,2]{2,1,0:T(2,128)(2,1)S(1)}, u32[]{:S(2)}, u32[]{:S(2)}) async-start(bf16[32,1,2]{2,1,0:T(2,128)(2,1)} %broadcast_select_fusion.14), calls=%async_computation.2 | async-start | bytes 32768 | tf_op jit(solution)/shard_map/all_to_all | solution.py:92
  50.9 12.4 %copy-start.42 = (s32[4]{0:T(128)S(1)}, s32[4]{0:T(128)}, u32[]{:S(2)}) copy-start(s32[4]{0:T(128)} %param.47) | copy-start | bytes 52
  50.9 15.7 %copy-start.9 = (bf16[1,64,1024]{2,1,0:T(8,128)(2,1)S(1)}, bf16[1,64,1024]{2,1,0:T(8,128)(2,1)}, u32[]{:S(2)}) copy-start(bf16[1,64,1024]{2,1,0:T(8,128)(2,1)} %param.52) | copy-start | bytes 393220
  50.9 16.5 %copy-start.5 = (bf16[1,2,64,1024]{3,2,1,0:T(8,128)(2,1)S(1)}, bf16[1,2,64,1024]{3,2,1,0:T(8,128)(2,1)}, u32[]{:S(2)}) copy-start(bf16[1,2,64,1024]{3,2,1,0:T(8,128)(2,1)} %param.51) | copy-start | bytes 786436
  50.9 17.6 %copy-start.34 = (bf16[1,64,128]{2,1,0:T(8,128)(2,1)S(1)}, bf16[1,64,128]{2,1,0:T(8,128)(2,1)}, u32[]{:S(2)}) copy-start(bf16[1,64,128]{2,1,0:T(8,128)(2,1)} %param.53) | copy-start | bytes 49156
  50.9 18.3 %copy-start.1 = (bf16[2,2,64,1024]{3,2,1,0:T(8,128)(2,1)S(1)}, bf16[2,2,64,1024]{3,2,1,0:T(8,128)(2,1)}, u32[]{:S(2)}) copy-start(bf16[2,2,64,1024]{3,2,1,0:T(8,128)(2,1)} %param.48) | copy-start | bytes 1572868
  58.0 584.4 %all-to-all-start.1 = ((bf16[32,2,128,2,128]{4,2,3,1,0:T(8,128)(2,1)}), bf16[32,2,128,2,128]{4,2,3,1,0:T(8,128)(2,1)}, u32[]{:S(2)}, u32[]{:S(2)}) async-start(bf16[32,2,128,2,128]{4,2,3,1,0:T(8,128)(2,1)} %broadcast_select_fusion.3), calls=%async_computation.1 | async-start | bytes 8388608 | tf_op jit(solution)/shard_map/all_to_all | solution.py:91
  63.3 296.2 %copy-start.2 = (bf16[4,64,1024]{2,1,0:T(8,128)(2,1)S(1)}, bf16[4,64,1024]{2,1,0:T(8,128)(2,1)}, u32[]{:S(2)}) copy-start(bf16[4,64,1024]{2,1,0:T(8,128)(2,1)} %param.39) | copy-start | bytes 1572868
  63.3 295.2 %all-reduce.10.cloned.1.call-start = ((), (), s32[]{:S(2)}) async-start(), calls=%async_computation.13 | async-start | bytes 3145728 | tf_op jit(solution)/shard_map/psum | solution.py:14
  67.5 293.5 %copy-start.49 = (s32[4,64]{1,0:T(4,128)S(1)}, s32[4,64]{1,0:T(4,128)}, u32[]{:S(2)}) copy-start(s32[4,64]{1,0:T(4,128)} %param.44) | copy-start | bytes 3076
  67.5 294.2 %copy-start.26 = (bf16[2,64,128]{2,1,0:T(8,128)(2,1)S(1)}, bf16[2,64,128]{2,1,0:T(8,128)(2,1)}, u32[]{:S(2)}) copy-start(bf16[2,64,128]{2,1,0:T(8,128)(2,1)} %param.50) | copy-start | bytes 98308
  68.4 293.3 %copy-start.10 = (bf16[4,64,2,128]{3,2,1,0:T(2,128)(2,1)S(1)}, bf16[4,64,2,128]{3,2,1,0:T(2,128)(2,1)}, u32[]{:S(2)}) copy-start(bf16[4,64,2,128]{3,2,1,0:T(2,128)(2,1)} %param.41) | copy-start | bytes 393220
  68.5 526.7 %all-reduce.8.cloned.1.call-start = ((), (), s32[]{:S(2)}) async-start(), calls=%async_computation.12 | async-start | bytes 131072 | tf_op jit(solution)/shard_map/psum | solution.py:14
  69.2 568.9 %all-gather.9.cloned.1.call-start = ((), (), s32[]{:S(2)}) async-start(), calls=%async_computation.8 | async-start | bytes 3538944 | tf_op jit(solution)/shard_map/all_gather | solution.py:105
  363.1 278.8 %copy-start.47 = (pred[32]{0:T(512)(128)(4,1)}, pred[32]{0:T(512)(128)(4,1)S(1)}, u32[]{:S(2)}) copy-start(pred[32]{0:T(512)(128)(4,1)S(1)} %iota_compare_fusion.10) | copy-start | bytes 100
  363.1 320.9 %copy-start.35 = (s32[2]{0:T(128)}, s32[2]{0:T(128)S(1)}, u32[]{:S(2)}) copy-start(s32[2]{0:T(128)S(1)} %get-tuple-element.220) | copy-start | bytes 28
  363.1 321.0 %copy-start.39 = (s32[2]{0:T(128)}, s32[2]{0:T(128)S(1)}, u32[]{:S(2)}) copy-start(s32[2]{0:T(128)S(1)} %get-tuple-element.219) | copy-start | bytes 28
  363.1 278.8 %copy-start.44 = (s32[1024]{0:T(1024)}, s32[1024]{0:T(1024)S(1)}, u32[]{:S(2)}) copy-start(s32[1024]{0:T(1024)S(1)} %pad_clamp_fusion.1) | copy-start | bytes 12292
  642.5 29.2 %all-to-all-start.4 = ((bf16[32,1,2]{2,1,0:T(2,128)(2,1)}), bf16[32,1,2]{2,1,0:T(2,128)(2,1)S(1)}, u32[]{:S(2)}, u32[]{:S(2)}) async-start(bf16[32,1,2]{2,1,0:T(2,128)(2,1)} %broadcast_select_fusion.13), calls=%async_computation.4 | async-start | bytes 32768 | tf_op jit(solution)/shard_map/all_to_all | solution.py:92
  671.6 10.1 copy-start.8
  671.6 106.2 %all-to-all-start.3 = ((bf16[32,2,128,2,128]{4,2,3,1,0:T(8,128)(2,1)}), bf16[32,2,128,2,128]{4,2,3,1,0:T(8,128)(2,1)}, u32[]{:S(2)}, u32[]{:S(2)}) async-start(bf16[32,2,128,2,128]{4,2,3,1,0:T(8,128)(2,1)} %broadcast_select_fusion.2), calls=%async_computation.3 | async-start | bytes 8388608 | tf_op jit(solution)/shard_map/all_to_all | solution.py:91
  681.7 71.3 %all-gather.11.cloned.1.call-start = ((), (), s32[]{:S(2)}) async-start(), calls=%async_computation.9 | async-start | bytes 3538944 | tf_op jit(solution)/shard_map/all_gather | solution.py:105
  682.3 75.3 %copy-start.32 = (bf16[1,64,128]{2,1,0:T(8,128)(2,1)S(1)}, bf16[1,64,128]{2,1,0:T(8,128)(2,1)}, u32[]{:S(2)}) copy-start(bf16[1,64,128]{2,1,0:T(8,128)(2,1)} %get-tuple-element.154) | copy-start | bytes 49156
  684.0 68.9 %copy-start.45 = (pred[32]{0:T(512)(128)(4,1)}, pred[32]{0:T(512)(128)(4,1)S(1)}, u32[]{:S(2)}) copy-start(pred[32]{0:T(512)(128)(4,1)S(1)} %iota_compare_fusion.9) | copy-start | bytes 100
  684.0 68.9 %copy-start.43 = (s32[1024]{0:T(1024)}, s32[1024]{0:T(1024)S(1)}, u32[]{:S(2)}) copy-start(s32[1024]{0:T(1024)S(1)} %pad_clamp_fusion) | copy-start | bytes 12292
  757.9 28.3 %copy-start.38 = (s32[2]{0:T(128)S(1)}, s32[2]{0:T(128)}, u32[]{:S(2)}) copy-start(s32[2]{0:T(128)} %copy-done.37) | copy-start | bytes 28
  777.9 32.4 %all-to-all-start.6 = ((bf16[32,1,2]{2,1,0:T(2,128)(2,1)}), bf16[32,1,2]{2,1,0:T(2,128)(2,1)S(1)}, u32[]{:S(2)}, u32[]{:S(2)}) async-start(bf16[32,1,2]{2,1,0:T(2,128)(2,1)} %broadcast_select_fusion.12), calls=%async_computation.6 | async-start | bytes 32768 | tf_op jit(solution)/shard_map/all_to_all | solution.py:92
  788.3 19.6 %copy-start.48 = (pred[32]{0:T(512)(128)(4,1)S(1)}, pred[32]{0:T(512)(128)(4,1)}, u32[]{:S(2)}) copy-start(pred[32]{0:T(512)(128)(4,1)} %copy-done.47) | copy-start | bytes 100
  810.2 10.7 copy-start.7
  810.8 106.2 %all-to-all-start.5 = ((bf16[32,2,128,2,128]{4,2,3,1,0:T(8,128)(2,1)}), bf16[32,2,128,2,128]{4,2,3,1,0:T(8,128)(2,1)}, u32[]{:S(2)}, u32[]{:S(2)}) async-start(bf16[32,2,128,2,128]{4,2,3,1,0:T(8,128)(2,1)} %broadcast_select_fusion.1), calls=%async_computation.5 | async-start | bytes 8388608 | tf_op jit(solution)/shard_map/all_to_all | solution.py:91
  820.8 4.0 copy-start.17
  820.8 4.0 copy-start.18
  820.8 4.6 copy-start.50
  820.8 8.5 copy-start.6
  820.8 71.1 %all-gather.13.cloned.1.call-start = ((), (), s32[]{:S(2)}) async-start(), calls=%async_computation.10 | async-start | bytes 3538944 | tf_op jit(solution)/shard_map/all_gather | solution.py:105
  822.4 129.0 %all-gather.15.cloned.1.call-start = ((), (), s32[]{:S(2)}) async-start(), calls=%async_computation.11 | async-start | bytes 3538944 | tf_op jit(solution)/shard_map/all_gather | solution.py:105
  824.8 4.5 copy-start.15
  829.4 66.1 %copy-start.28 = (f32[64,6]{0,1:T(8,128)S(1)}, f32[64,6]{0,1:T(8,128)}, u32[]{:S(2)}) copy-start(f32[64,6]{0,1:T(8,128)} %get-tuple-element.208) | copy-start | bytes 4612
  830.0 65.7 %copy-start.20 = (bf16[64,6]{1,0:T(8,128)(2,1)S(1)}, bf16[64,6]{1,0:T(8,128)(2,1)}, u32[]{:S(2)}) copy-start(bf16[64,6]{1,0:T(8,128)(2,1)} %copy.116) | copy-start | bytes 2308
  830.0 66.0 %copy-start.31 = (bf16[1,64,128]{2,1,0:T(8,128)(2,1)S(1)}, bf16[1,64,128]{2,1,0:T(8,128)(2,1)}, u32[]{:S(2)}) copy-start(bf16[1,64,128]{2,1,0:T(8,128)(2,1)} %get-tuple-element.155) | copy-start | bytes 49156
  830.0 66.0 %copy-start.16 = (bf16[64,2,128]{2,0,1:T(8,128)(2,1)S(1)}, bf16[64,2,128]{2,0,1:T(8,128)(2,1)}, u32[]{:S(2)}) copy-start(bf16[64,2,128]{2,0,1:T(8,128)(2,1)} %copy-done.15) | copy-start | bytes 98308
  830.0 66.2 %copy-start.22 = (bf16[64,1,128]{2,0,1:T(8,128)(2,1)S(1)}, bf16[64,1,128]{2,0,1:T(8,128)(2,1)}, u32[]{:S(2)}) copy-start(bf16[64,1,128]{2,0,1:T(8,128)(2,1)} %slice.517) | copy-start | bytes 49156
  896.3 21.7 %copy-start.40 = (s32[2]{0:T(128)S(1)}, s32[2]{0:T(128)}, u32[]{:S(2)}) copy-start(s32[2]{0:T(128)} %copy-done.39) | copy-start | bytes 28
  920.0 19.8 %copy-start.46 = (pred[32]{0:T(512)(128)(4,1)S(1)}, pred[32]{0:T(512)(128)(4,1)}, u32[]{:S(2)}) copy-start(pred[32]{0:T(512)(128)(4,1)} %copy-done.45) | copy-start | bytes 100
  942.2 7.8 copy-start.14
  942.2 7.9 copy-start.3
  942.2 8.2 copy-start.4
  942.2 8.4 copy-start.13
  942.2 8.9 copy-start.12
  942.2 103.8 %all-to-all-start.7 = ((bf16[32,2,128,2,128]{4,2,3,1,0:T(8,128)(2,1)}), bf16[32,2,128,2,128]{4,2,3,1,0:T(8,128)(2,1)}, u32[]{:S(2)}, u32[]{:S(2)}) async-start(bf16[32,2,128,2,128]{4,2,3,1,0:T(8,128)(2,1)} %broadcast_select_fusion), calls=%async_computation.7 | async-start | bytes 8388608 | tf_op jit(solution)/shard_map/all_to_all | solution.py:91
  950.4 4.7 copy-start.27
  950.4 4.8 copy-start.19
  950.9 4.7 copy-start.30
  950.9 4.8 copy-start.21
  950.9 5.0 copy-start.11
  956.3 10.0 copy-start.25
  970.9 10.0 copy-start.24
  985.5 5.5 copy-start
  990.9 6.8 copy-start.23
  997.7 49.2 %copy-start.36 = (s32[2]{0:T(128)S(1)}, s32[2]{0:T(128)}, u32[]{:S(2)}) copy-start(s32[2]{0:T(128)} %copy-done.35) | copy-start | bytes 28
  (2 other events, 3.3 us)
Sparse Core Ops, SparseCore 0:
  68.6 289.8 all-reduce.9
  361.4 233.7 all-reduce.7
  597.0 41.1 all-gather.8
  684.0 68.9 all-gather.10
  823.1 68.7 all-gather.12
  893.6 47.7 all-gather.14
